TPU v7x, 128 devices: a whole 4x4x4 slice. The times are simulated.
128 devices in a mesh: dp: 128 (over z, y, x, core).
Axes of the slice: x: 4, y: 4, z: 4, core: 2. Of those that a mesh axis runs over, the one named last changes fastest.
Arguments:
- gradient: float32 [128, 16384, 128], P('dp'), may hold values from -6 to 6
- residual: float32 [128, 16384, 128], P('dp'), may hold values from -5 to 5
- weights: float32 [16384, 128], replicated, may hold values from -6 to 6
- momentum: float32 [16384, 128], replicated, may hold values from -6 to 6
- sel_idx: int32 [128, 128, 4], replicated, may hold values from 0 to 16383, as said below
- sel_count: int32 [128, 128], replicated, may hold values from 1 to 4, as said below
- gath_idx: int32 [128, 8], replicated, may hold values from 0 to 16383, as said below
- gath_count: int32 [128], replicated, may hold values from 6 to 8, as said below
Outputs:
- new_weights: float32 [16384, 128], replicated
- new_momentum: float32 [16384, 128], replicated
- new_residual: float32 [128, 16384, 128], P('dp')
Inputs may be any that keep to these rules, and one draw needn't show every extreme that they name: Owners' regions are consecutive runs of blocks in owner order covering all 16384 blocks, each of 64 to 192 blocks, some of exactly 192. All 4 entries of sel_idx[s, o] are distinct entries of gath_idx[o], those at or beyond sel_count[s, o] included. `sel_count`: some owner receives exactly 4 used slots from every replica. All 8 entries of gath_idx[o] are distinct blocks of owner o's region. `gath_count`: some owner lists exactly 8 blocks.
All inputs are finite; a program needn't handle non-finite values.
Results may differ from a plain program's by a relative error of at most 0.00002.
Values sent between devices are 32-bit elements; how exact they have to be, the bound alone decides.
No kernel may reach another device: no remote copies, remote signals or barrier semaphores. Data moves between devices by JAX's collectives and lax.ppermute only.
A program may use at most 192 MiB of HBM per device.

v0:
```python
import jax
import jax.numpy as jnp
from jax import lax
from jax.sharding import PartitionSpec as P

momentum_coef = 0.9
learning_rate = 0.05


def local(gradient, residual, weights, momentum, sel_idx, sel_count, gath_idx, gath_count):
    my_rank = lax.axis_index("dp")
    accumulated = gradient[0] + residual[0]
    block_count, block_len = accumulated.shape
    capacity = sel_idx.shape[2]
    list_len = gath_idx.shape[1]
    slot_ids = jnp.arange(capacity, dtype=jnp.int32)
    my_ids = lax.dynamic_index_in_dim(sel_idx, my_rank, 0, keepdims=False)
    my_counts = lax.dynamic_index_in_dim(sel_count, my_rank, 0, keepdims=False)
    my_valid = (slot_ids[None, :] < my_counts[:, None]).astype(jnp.float32)
    list_slots = jnp.arange(list_len, dtype=jnp.int32)
    list_valid = (list_slots[None, :] < gath_count[:, None]).astype(jnp.float32)
    listed = (
        jnp.zeros((block_count,), jnp.float32).at[gath_idx.reshape(-1)].max(list_valid.reshape(-1))
    )
    my_mask = (
        jnp.zeros((block_count,), jnp.float32).at[my_ids.reshape(-1)].max(my_valid.reshape(-1))
    )
    summed = lax.psum(accumulated * my_mask[:, None], "dp")
    update = summed * listed[:, None]
    new_momentum = momentum_coef * momentum + update
    new_weights = weights - learning_rate * new_momentum
    new_residual = (accumulated * (1.0 - my_mask * listed)[:, None])[None]
    return (new_weights, new_momentum, new_residual)


def solution(mesh):
    placed = (P("dp", None, None), P("dp", None, None), P(), P(), P(), P(), P(), P())
    return jax.shard_map(
        local,
        mesh=mesh,
        in_specs=placed,
        out_specs=(P(), P(), P("dp", None, None)),
        check_vma=False,
    )
```

profile of v0, /device:TPU:1, one launch (start us, length us, event | category | flops | bytes accessed | tf_op | source)
XLA Modules:
  0.0 215.8 jit_solution(15140368496560927797)
XLA Ops:
  7.2 0.0 copy-start
  7.2 0.0 all-reduce.2.cloned.1.call-start
  7.2 0.9 copy-done
  8.1 0.1 copy.11
  8.2 0.1 reshape.93
  8.4 0.7 dynamic-slice_bitcast_fusion
  9.1 0.1 fusion
  9.1 0.1 reshape.101
  9.3 4.0 %scatter_custom_fusion = f32[16384]{0:T(1024)S(1)} fusion(s32[512]{0:T(512)S(1)} %bitcast.7, f32[512]{0:T(512)S(1)} %reshape.101, f32[]{:T(128)} %constant.9.clone.1), kind=kCustom, calls=%fused_computation.13 | custom fusion | flops 512 | bytes 65540 | tf_op jit(solution)/shard_map/scatter-max | solution.py:26
  13.3 13.3 %bitcast_multiply_fusion = f32[16384,128]{1,0:T(8,128)} fusion(f32[16384]{0:T(1024)S(1)} %scatter_custom_fusion, f32[1,16384,128]{2,1,0:T(8,128)} %param.8, f32[1,16384,128]{2,1,0:T(8,128)} %param.9), kind=kLoop, calls=%fused_computation.2 | loop fusion | flops 4194304 | bytes 25231360 | tf_op jit(solution)/shard_map/mul | solution.py:28
  26.6 0.0 copy-start.2
  26.6 0.0 copy-start.3
  26.6 0.0 all-reduce.2.cloned.1.call-update
  26.6 0.7 copy-done.2
  27.2 0.1 copy.12
  27.3 0.1 reshape.94
  27.5 0.0 copy-done.3
  27.5 0.1 fusion.1
  27.6 0.1 reshape.109
  27.6 7.5 %scatter_custom_fusion.1 = f32[16384]{0:T(1024)S(1)} fusion(s32[1024]{0:T(1024)S(1)} %bitcast.6, f32[1024]{0:T(1024)S(1)} %reshape.109, f32[]{:T(128)} %constant.9.clone.1), kind=kCustom, calls=%fused_computation.11 | custom fusion | flops 1024 | bytes 65540 | tf_op jit(solution)/shard_map/scatter-max | solution.py:23
  35.1 13.2 %broadcast_multiply_fusion = f32[1,16384,128]{2,1,0:T(8,128)} fusion(f32[16384]{0:T(1024)S(1)} %multiply_subtract_fusion.1, f32[1,16384,128]{2,1,0:T(8,128)} %param.8, f32[1,16384,128]{2,1,0:T(8,128)} %param.9), kind=kLoop, calls=%fused_computation.5 | loop fusion | flops 4194304 | bytes 25231360 | tf_op jit(solution)/shard_map/mul | solution.py:32
  48.3 142.8 %all-reduce.2.cloned.1.call-done = f32[16384,128]{1,0:T(8,128)} async-done(((f32[16384,128]{1,0:T(8,128)}), f32[16384,128]{1,0:T(8,128)}) %all-reduce.2.cloned.1.call-update) | async-done | bytes 8388624 | tf_op jit(solution)/shard_map/psum | solution.py:28
  191.2 0.0 copy-start.1
  191.2 17.8 %multiply_subtract_fusion = (f32[16384,128]{1,0:T(8,128)}, f32[16384,128]{1,0:T(8,128)}) fusion(f32[16384,128]{1,0:T(8,128)} %param.10, f32[16384,128]{1,0:T(8,128)} %all-reduce.2.cloned.1.call-done, f32[16384]{0:T(1024)S(1)} %scatter_custom_fusion.1, f32[16384,128]{1,0:T(8,128)} %param.11), kind=kLoop, calls=%fused_computation.3 | loop fusion | flops 10485760 | bytes 42008576 | tf_op jit(solution)/shard_map/sub | solution.py:31
  209.0 0.0 copy-done.1
  (4 shorter events, 0.0 us)
Async XLA Ops:
  7.2 1.0 copy-start
  7.2 184.0 %all-reduce.2.cloned.1.call-start = ((), (), s32[]{:S(2)}) async-start(), calls=%async_computation | async-start | bytes 16777216 | tf_op jit(solution)/shard_map/psum | solution.py:28
  26.6 0.7 copy-start.2
  26.6 0.9 copy-start.3
  191.2 17.8 %copy-start.1 = (s32[128,128,4]{1,2,0:T(4,128)S(1)}, s32[128,128,4]{1,2,0:T(4,128)}, u32[]{:S(2)}) copy-start(s32[128,128,4]{1,2,0:T(4,128)} %param.12) | copy-start | bytes 786436
Sparse Core Ops, SparseCore 0:
  26.7 164.4 all-reduce.1
where the time goes:
time: 216 us
  waiting for transfers between devices  143 us (66%)
  other arithmetic  55.9 us (26%)
  between operations  14.1 us (7%)
  local copies, waits for them, and re-layouts  2.88 us (1%)
    psum x1, waiting for transfers between devices, local(): summed = lax.psum(accumulated * my_mask[:, None], 'dp')  143 us
    sub x1, other arithmetic, local(): new_weights = weights - learning_rate * new_momentum  17.8 us
    mul x1, other arithmetic, local(): summed = lax.psum(accumulated * my_mask[:, None], 'dp')  13.3 us
    mul x1, other arithmetic, local(): new_residual = (accumulated * (1.0 - my_mask * listed)[:, None])[None]  13.2 us
    another operation x1, other arithmetic, local(): jnp.zeros((block_count,), jnp.float32).at[gath_idx.reshape(-1)]  7.46 us
  transfers between devices with their start and end apart: 1, of which 1 were waited for; matrix products, arithmetic and copies ran while one was open for 10% of the time, Pallas kernels for 0%

commit v1 on v0

v1 whole, which is shorter than its diff:
```python
import jax
import jax.numpy as jnp
from jax import lax
from jax.experimental import pallas as pl
from jax.experimental.pallas import tpu as pltpu
from jax.sharding import PartitionSpec as P

momentum_coef = 0.9
learning_rate = 0.05
F32 = jnp.float32
VMEM = pl.BlockSpec(memory_space=pltpu.VMEM)
HBM = pl.BlockSpec(memory_space=pltpu.HBM)
CHUNKS = 8
VMEM_ALL = 67_000_000


def cost(nbytes):
    return pl.CostEstimate(flops=0, transcendentals=0, bytes_accessed=nbytes)


def gather_rows(sel_ref, grad_ref, res_ref, out_ref, ids, buf, id_sem, sem):
    cap, owners = ids.shape
    rows = cap * owners
    copy = pltpu.make_async_copy(sel_ref.at[lax.axis_index("dp")], ids, id_sem)
    copy.start()
    copy.wait()

    def issue(o, carry):
        for c in range(cap):
            block = ids[c, o]
            slot = o * cap + c
            pltpu.make_async_copy(grad_ref.at[pl.ds(block, 1)], buf.at[0, pl.ds(slot, 1)], sem).start()
            pltpu.make_async_copy(res_ref.at[pl.ds(block, 1)], buf.at[1, pl.ds(slot, 1)], sem).start()
        return carry

    lax.fori_loop(0, owners, issue, 0, unroll=4)
    pltpu.make_async_copy(grad_ref.at[pl.ds(0, rows)], buf.at[0], sem).wait()
    pltpu.make_async_copy(res_ref.at[pl.ds(0, rows)], buf.at[1], sem).wait()
    out_ref[...] = buf[0] + buf[1]


def reduce_rows(hot_ref, rows_ref, after_ref, out_ref):
    del after_ref
    sums = jnp.dot(hot_ref[...], rows_ref[...], precision=lax.Precision.HIGHEST, preferred_element_type=F32)
    slots = sums.shape[0]
    copies = out_ref.shape[0] // slots
    out_ref[...] = jnp.broadcast_to(sums[None], (copies,) + sums.shape).reshape(out_ref.shape)


def residual_pass(
    sel_ref, scount_ref, gath_ref, gcount_ref, grad_ref, res_ref, after_ref, out_ref, ids_v, cnt_v, ids_s, a, b, in_sem, out_sem, sem
):
    del after_ref
    blocks = grad_ref.shape[0]
    step = blocks // CHUNKS
    me = lax.axis_index("dp")
    ins = []
    for k in range(CHUNKS):
        part = pl.ds(k * step, step)
        ins.append(
            (
                pltpu.make_async_copy(grad_ref.at[part], a.at[part], in_sem.at[0, k]),
                pltpu.make_async_copy(res_ref.at[part], b.at[part], in_sem.at[1, k]),
            )
        )
        ins[-1][0].start()
        ins[-1][1].start()
    first = pltpu.make_async_copy(sel_ref.at[me], ids_v, sem.at[0])
    second = pltpu.make_async_copy(scount_ref.at[pl.ds(me, 1)], cnt_v, sem.at[1])
    first.start()
    second.start()
    first.wait()
    second.wait()
    ids = ids_v[...]
    cap, owners = ids.shape
    sent = lax.broadcasted_iota(jnp.int32, (cap, owners), 0) < jnp.broadcast_to(cnt_v[...], (cap, owners))
    listed = jnp.zeros((cap, owners), jnp.bool_)
    for k in range(gath_ref.shape[0]):
        same = ids == jnp.broadcast_to(gath_ref[pl.ds(k, 1), :], (cap, owners))
        listed = listed | (same & (jnp.broadcast_to(gcount_ref[...], (cap, owners)) > k))
    ids_v[...] = jnp.where(sent & listed, ids, blocks)
    third = pltpu.make_async_copy(ids_v, ids_s, sem.at[0])
    third.start()
    third.wait()
    for k in range(CHUNKS):
        part = pl.ds(k * step, step)
        ins[k][0].wait()
        ins[k][1].wait()
        a[part, :] = a[part, :] + b[part, :]
    zero = jnp.zeros((1, a.shape[1]), F32)

    def clear(o, carry):
        for c in range(cap):
            a[pl.ds(ids_s[c, o], 1), :] = zero
        return carry

    lax.fori_loop(0, owners, clear, 0, unroll=4)
    outs = []
    for k in range(CHUNKS):
        part = pl.ds(k * step, step)
        outs.append(pltpu.make_async_copy(a.at[part], out_ref.at[part], out_sem.at[k]))
        outs[-1].start()
    for copy in outs:
        copy.wait()


def base_pass(gath_ref, w_ref, m_ref, after_ref, nw_ref, nm_ref, wrow_ref, mrow_ref, w, m, in_sem, out_sem):
    del after_ref
    blocks = w_ref.shape[0]
    step = blocks // CHUNKS
    list_len, owners = gath_ref.shape
    ins = []
    for k in range(CHUNKS):
        part = pl.ds(k * step, step)
        ins.append(
            (
                pltpu.make_async_copy(m_ref.at[part], m.at[part], in_sem.at[0, k]),
                pltpu.make_async_copy(w_ref.at[part], w.at[part], in_sem.at[1, k]),
            )
        )
        ins[-1][0].start()
        ins[-1][1].start()
    outs = []
    for k in range(CHUNKS):
        part = pl.ds(k * step, step)
        ins[k][0].wait()
        ins[k][1].wait()
        base = momentum_coef * m[part, :]
        m[part, :] = base
        w[part, :] = w[part, :] - learning_rate * base
        outs.append(pltpu.make_async_copy(m.at[part], nm_ref.at[part], out_sem.at[0, k]))
        outs.append(pltpu.make_async_copy(w.at[part], nw_ref.at[part], out_sem.at[1, k]))
        outs[-1].start()
        outs[-2].start()

    def take(o, carry):
        for k in range(list_len):
            block = gath_ref[k, o]
            slot = o * list_len + k
            mrow_ref[pl.ds(slot, 1), :] = m[pl.ds(block, 1), :]
            wrow_ref[pl.ds(slot, 1), :] = w[pl.ds(block, 1), :]
        return carry

    lax.fori_loop(0, owners, take, 0, unroll=2)
    for copy in outs:
        copy.wait()


def patch(gath_ref, u_ref, wrow_ref, mrow_ref, nw_in, nm_in, nw_ref, nm_ref, wrow, mrow, sem):
    rows = u_ref.shape[0]
    list_len, owners = gath_ref.shape
    u = u_ref[...]
    mrow[...] = mrow_ref[...] + u
    wrow[...] = wrow_ref[...] - learning_rate * u

    def issue(o, carry):
        for k in range(list_len):
            block = gath_ref[k, o]
            slot = o * list_len + k
            pltpu.make_async_copy(mrow.at[pl.ds(slot, 1)], nm_ref.at[pl.ds(block, 1)], sem.at[0]).start()
            pltpu.make_async_copy(wrow.at[pl.ds(slot, 1)], nw_ref.at[pl.ds(block, 1)], sem.at[1]).start()
        return carry

    lax.fori_loop(0, owners, issue, 0, unroll=2)
    pltpu.make_async_copy(mrow, nm_ref.at[pl.ds(0, rows)], sem.at[0]).wait()
    pltpu.make_async_copy(wrow, nw_ref.at[pl.ds(0, rows)], sem.at[1]).wait()


def local(gradient, residual, weights, momentum, sel_idx, sel_count, gath_idx, gath_count):
    me = lax.axis_index("dp")
    grad, res = gradient[0], residual[0]
    blocks, width = grad.shape
    owners, cap = sel_idx.shape[1:]
    list_len = gath_idx.shape[1]
    sel_t = jnp.transpose(sel_idx, (0, 2, 1))
    gath_t = jnp.transpose(gath_idx, (1, 0))
    smem = pl.BlockSpec(memory_space=pltpu.SMEM)
    full = jax.ShapeDtypeStruct((blocks, width), F32)
    dma = pltpu.SemaphoreType.DMA

    rows = pl.pallas_call(
        gather_rows,
        out_shape=jax.ShapeDtypeStruct((owners * cap, width), F32),
        in_specs=[HBM, HBM, HBM],
        out_specs=VMEM,
        scratch_shapes=[
            pltpu.SMEM((cap, owners), jnp.int32),
            pltpu.VMEM((2, owners * cap, width), F32),
            dma(()),
            dma(()),
        ],
        compiler_params=pltpu.CompilerParams(vmem_limit_bytes=VMEM_ALL),
        cost_estimate=cost(owners * cap * width * 8),
        name="gather_rows",
    )(sel_t, grad, res)
    got = lax.all_to_all(rows.reshape(owners, cap, width), "dp", 0, 0, tiled=True)

    mine = lax.dynamic_index_in_dim(sel_idx, me, 1, keepdims=False)
    mine_count = lax.dynamic_index_in_dim(sel_count, me, 1, keepdims=False)
    my_list = lax.dynamic_index_in_dim(gath_idx, me, 0, keepdims=False)
    my_listed = lax.dynamic_index_in_dim(gath_count, me, 0, keepdims=False)
    hot = (
        (mine[None] == my_list[:, None, None])
        & (jnp.arange(cap)[None, None, :] < mine_count[None, :, None])
        & (jnp.arange(list_len)[:, None, None] < my_listed)
    )
    hot = hot.astype(F32).reshape(list_len, owners * cap)

    new_residual = pl.pallas_call(
        residual_pass,
        out_shape=full,
        in_specs=[HBM, HBM, VMEM, VMEM, HBM, HBM, HBM],
        out_specs=HBM,
        scratch_shapes=[
            pltpu.VMEM((cap, owners), jnp.int32),
            pltpu.VMEM((1, owners), jnp.int32),
            pltpu.SMEM((cap, owners), jnp.int32),
            pltpu.VMEM((blocks + 8, width), F32),
            pltpu.VMEM((blocks, width), F32),
            dma((2, CHUNKS)),
            dma((CHUNKS,)),
            dma((2,)),
        ],
        cost_estimate=cost(blocks * width * 12),
        name="residual_pass",
    )(sel_t, sel_count, gath_t, gath_count.reshape(1, owners), grad, res, rows)

    shared = pl.pallas_call(
        reduce_rows,
        out_shape=jax.ShapeDtypeStruct((owners * list_len, width), F32),
        in_specs=[VMEM, VMEM, HBM],
        out_specs=VMEM,
        compiler_params=pltpu.CompilerParams(vmem_limit_bytes=VMEM_ALL),
        cost_estimate=cost(owners * list_len * width * 8),
        name="reduce_rows",
    )(hot, got.reshape(owners * cap, width), new_residual)
    sums = lax.all_to_all(shared.reshape(owners, list_len, width), "dp", 0, 0, tiled=True)

    listed_rows = jax.ShapeDtypeStruct((owners * list_len, width), F32)
    nw, nm, wrow, mrow = pl.pallas_call(
        base_pass,
        out_shape=(full, full, listed_rows, listed_rows),
        in_specs=[smem, HBM, HBM, HBM],
        out_specs=(HBM, HBM, VMEM, VMEM),
        scratch_shapes=[
            pltpu.VMEM((blocks, width), F32),
            pltpu.VMEM((blocks, width), F32),
            dma((2, CHUNKS)),
            dma((2, CHUNKS)),
        ],
        cost_estimate=cost(blocks * width * 16),
        name="base_pass",
    )(gath_t, weights, momentum, shared)

    new_weights, new_momentum = pl.pallas_call(
        patch,
        out_shape=(full, full),
        in_specs=[smem, VMEM, VMEM, VMEM, HBM, HBM],
        out_specs=(HBM, HBM),
        scratch_shapes=[
            pltpu.VMEM((owners * list_len, width), F32),
            pltpu.VMEM((owners * list_len, width), F32),
            dma((2,)),
        ],
        input_output_aliases={4: 0, 5: 1},
        compiler_params=pltpu.CompilerParams(vmem_limit_bytes=VMEM_ALL),
        cost_estimate=cost(owners * list_len * width * 16),
        name="patch",
    )(gath_t, sums.reshape(owners * list_len, width), wrow, mrow, nw, nm)
    return new_weights, new_momentum, new_residual[None]


def solution(mesh):
    placed = (P("dp", None, None), P("dp", None, None), P(), P(), P(), P(), P(), P())
    return jax.shard_map(
        local,
        mesh=mesh,
        in_specs=placed,
        out_specs=(P(), P(), P("dp", None, None)),
        check_vma=False,
    )
```

time: 216 us -> 74.6 us (0.35)
  waiting for transfers between devices: 143 us -> 0.01 us
  other arithmetic: 55.9 us -> 1.34 us
  Pallas kernels: 0 us -> 44.3 us
  starting transfers between devices: 0.04 us -> 22.2 us
  between operations: 14.1 us -> 0.75 us
  local copies, waits for them, and re-layouts: 2.88 us -> 5.56 us
    psum x1 -> x0, waiting for transfers between devices: 143 us -> none  [local(): summed = lax.psum(accumulated * my_mask[:, None], 'dp')]
    pallas_call x0 -> x5, Pallas kernels: none -> 44.3 us  [the longest x1 14.4 us: local(): pl.pallas_call(base_pass, out_shape=(full, full, listed_rows, listed_rows...]
    mul x2 -> x0, other arithmetic: 26.5 us -> none  [the longest x1 13.3 us: local(): summed = lax.psum(accumulated * my_mask[:, None], 'dp')]
    all_to_all x0 -> x2, starting transfers between devices: none -> 22.2 us  [the longest x1 12 us: local(): lax.all_to_all(rows.reshape(owners, cap, width), 'dp', 0, 0, tiled=True)]
    sub x2 -> x0, other arithmetic: 17.8 us -> none  [the longest x1 17.8 us: local(): new_weights = weights - learning_rate * new_momentum]
    another operation x2 -> x0, other arithmetic: 11.5 us -> none  [the longest x1 7.46 us: local(): jnp.zeros((block_count,), jnp.float32).at[gath_idx.reshape(-1)]]
    dynamic_slice x2 -> x4, local copies, waits for them, and re-layouts: 0.12 us -> 5.13 us  [the longest x1 3.34 us: local(): mine = lax.dynamic_index_in_dim(sel_idx, me, 1, keepdims=False)]
  transfers between devices with their start and end apart: 1 -> 2, of which waited for: 1 -> 0; matrix products, arithmetic and copies ran while one was open for 10% -> 9% of each run, Pallas kernels for 0% -> 36%
where the time goes in v1:
time: 74.6 us; the launch traced here: 74.1 us
  Pallas kernels  44.3 us (59%)
  starting transfers between devices  22.2 us (30%)
  local copies, waits for them, and re-layouts  5.56 us (7%)
  other arithmetic  1.34 us (2%)
  between operations  0.75 us (1%)
    pallas_call x1, Pallas kernels, local(): pl.pallas_call(base_pass, out_shape=(full, full, listed_rows, listed_rows...  14.4 us
    pallas_call x1, Pallas kernels, local(): pl.pallas_call(residual_pass, out_shape=full, in_specs=[HBM, HBM, VMEM, V...  12 us
    all_to_all x1, starting transfers between devices, local(): lax.all_to_all(rows.reshape(owners, cap, width), 'dp', 0, 0, tiled=True)  12 us
    all_to_all x1, starting transfers between devices, local(): lax.all_to_all(shared.reshape(owners, list_len, width), 'dp', 0, 0, tiled...  10.2 us
    pallas_call x1, Pallas kernels, local(): pl.pallas_call(patch, out_shape=(full, full), in_specs=[smem, VMEM, VMEM,...  9.56 us
    pallas_call x1, Pallas kernels, local(): pl.pallas_call(gather_rows, out_shape=jax.ShapeDtypeStruct((owners * cap,...  6.37 us
    dynamic_slice x1, local copies, waits for them, and re-layouts, local(): mine = lax.dynamic_index_in_dim(sel_idx, me, 1, keepdims=False)  3.34 us
    pallas_call x1, Pallas kernels, local(): pl.pallas_call(reduce_rows, out_shape=jax.ShapeDtypeStruct((owners * list...  2.02 us
  transfers between devices with their start and end apart: 2, of which 0 were waited for; matrix products, arithmetic and copies ran while one was open for 9% of the time, Pallas kernels for 36%

profile of v1, /device:TPU:1, one launch (start us, length us, event | category | flops | bytes accessed | tf_op | source)
XLA Modules:
  0.0 74.1 jit_solution(16346682752346933257)
XLA Ops:
  0.6 0.0 copy-start.1
  0.6 0.0 copy-start
  0.7 6.4 %gather_rows.1.after_ref = f32[512,128]{1,0:T(8,128)} custom-call(s32[128,4,128]{2,1,0:T(4,128)} %bitcast.19, f32[16384,128]{1,0:T(8,128)} %bitcast.13, f32[16384,128]{1,0:T(8,128)} %bitcast.15), custom_call_target="tpu_custom_call" | custom-call | bytes 524288 | tf_op jit(solution)/shard_map/gather_rows/pallas_call | solution.py:181
  7.0 12.0 %all-to-all-start = ((f32[128,4,128]{2,1,0:T(4,128)}), f32[128,4,128]{2,1,0:T(4,128)}, u32[]{:S(2)}, u32[]{:S(2)}) async-start(f32[128,4,128]{2,1,0:T(4,128)} %bitcast.21), calls=%async_computation | async-start | bytes 524288 | tf_op jit(solution)/shard_map/all_to_all | solution.py:196
  19.0 0.0 copy-done.1
  19.0 0.6 dynamic_slice.22
  19.6 0.6 iota_compare_fusion
  20.2 0.0 copy-done
  20.3 0.2 dynamic-slice_reduce_fusion.2
  20.4 3.3 %dynamic-slice_reduce_fusion = s32[128,4]{1,0:T(8,128)S(1)} fusion(s32[128,128,4]{1,2,0:T(4,128)} %param.12, s32[]{:T(128)S(6)} %select_n.10), kind=kLoop, calls=%fused_computation | loop fusion | bytes 4100 | tf_op jit(solution)/shard_map/jit(dynamic_index_in_dim)/dynamic_slice | solution.py:198
  23.8 0.1 eq.18
  23.9 1.0 %dynamic-slice_reduce_fusion.1 = s32[128]{0:T(128)S(1)} fusion(s32[128,128]{1,0:T(8,128)} %scount_ref.1, s32[]{:T(128)S(6)} %select_n.10), kind=kLoop, calls=%fused_computation.1 | loop fusion | bytes 1028 | tf_op jit(solution)/shard_map/jit(dynamic_index_in_dim)/dynamic_slice | solution.py:199
  24.9 0.1 lt.46
  25.0 0.1 lt.47
  25.1 0.1 lt.45
  25.3 12.0 %residual_pass.1.after_ref = f32[16384,128]{1,0:T(8,128)} custom-call(s32[128,4,128]{2,1,0:T(4,128)} %bitcast.20, s32[128,128]{1,0:T(8,128)} %scount_ref.1, s32[8,128]{1,0:T(8,128)} %bitcast.22, s32[1,128]{1,0:T(1,128)} %bitcast.25, f32[16384,128]{1,0:T(8,128)} %bitcast.14, f32[16384,128]{1,0:T(8,128)} %bitcast.16, f32[512,128]{1,0:T(8,128)} %gather_rows.1.after_ref), custom_call_target="tpu_custom_call" | custom-call | bytes 25165824 | tf_op jit(solution)/shard_map/residual_pass/pallas_call | solution.py:209
  37.2 0.7 and_convert_fusion.hot_ref
  37.9 0.0 all-to-all-done
  37.9 2.0 %reduce_rows.1.after_ref = f32[1024,128]{1,0:T(8,128)} custom-call(f32[8,512]{1,0:T(8,128)} %and_convert_fusion.hot_ref, f32[512,128]{1,0:T(8,128)} %bitcast.6.rows_ref, f32[16384,128]{1,0:T(8,128)} %residual_pass.1.after_ref), custom_call_target="tpu_custom_call" | custom-call | bytes 1048576 | tf_op jit(solution)/shard_map/reduce_rows/pallas_call | solution.py:228
  39.9 10.2 %all-to-all-start.1 = ((f32[128,8,128]{2,1,0:T(8,128)}), f32[128,8,128]{2,1,0:T(8,128)}, u32[]{:S(2)}, u32[]{:S(2)}) async-start(f32[128,8,128]{2,1,0:T(8,128)} %bitcast.18), calls=%async_computation.1 | async-start | bytes 1048576 | tf_op jit(solution)/shard_map/all_to_all | solution.py:237
  50.2 14.4 %base_pass.1 = (f32[16384,128]{1,0:T(8,128)}, f32[16384,128]{1,0:T(8,128)}, f32[1024,128]{1,0:T(8,128)}, f32[1024,128]{1,0:T(8,128)}) custom-call(s32[8,128]{1,0:T(8,128)} %bitcast.23, f32[16384,128]{1,0:T(8,128)} %w_ref.1, f32[16384,128]{1,0:T(8,128)} %m_ref.1, f32[1024,128]{1,0:T(8,128)} %reduce_rows.1.after_ref), custom_call_target="tpu_custom_call" | custom-call | bytes 33554432 | tf_op jit(solution)/shard_map/base_pass/pallas_call | solution.py:240
  64.5 0.0 all-to-all-done.1
  64.5 9.6 %patch.1 = (f32[16384,128]{1,0:T(8,128)}, f32[16384,128]{1,0:T(8,128)}) custom-call(s32[8,128]{1,0:T(8,128)} %bitcast.24, f32[1024,128]{1,0:T(8,128)} %bitcast.9.u_ref, f32[1024,128]{1,0:T(8,128)} %get-tuple-element.9.wrow_ref, f32[1024,128]{1,0:T(8,128)} %get-tuple-element.10.mrow_ref, ...), custom_call_target="tpu_custom_call", output_to_operand_aliasing={{0}: (4, {}), {1}: (5, {})} | custom-call | bytes 2097152 | tf_op jit(solution)/shard_map/patch/pallas_call | solution.py:255
  (2 shorter events, 0.0 us)
Async XLA Ops:
  0.6 18.4 %copy-start.1 = (s32[128]{0:T(128)S(1)}, s32[128]{0:T(128)}, u32[]{:S(2)}) copy-start(s32[128]{0:T(128)} %param.15) | copy-start | bytes 1540
  0.6 19.6 %copy-start = (s32[128,8]{0,1:T(8,128)S(1)}, s32[128,8]{0,1:T(8,128)}, u32[]{:S(2)}) copy-start(s32[128,8]{0,1:T(8,128)} %param.14) | copy-start | bytes 12292
  7.0 30.9 %all-to-all-start = ((f32[128,4,128]{2,1,0:T(4,128)}), f32[128,4,128]{2,1,0:T(4,128)}, u32[]{:S(2)}, u32[]{:S(2)}) async-start(f32[128,4,128]{2,1,0:T(4,128)} %bitcast.21), calls=%async_computation | async-start | bytes 524288 | tf_op jit(solution)/shard_map/all_to_all | solution.py:196
  39.9 24.6 %all-to-all-start.1 = ((f32[128,8,128]{2,1,0:T(8,128)}), f32[128,8,128]{2,1,0:T(8,128)}, u32[]{:S(2)}, u32[]{:S(2)}) async-start(f32[128,8,128]{2,1,0:T(8,128)} %bitcast.18), calls=%async_computation.1 | async-start | bytes 1048576 | tf_op jit(solution)/shard_map/all_to_all | solution.py:237

commit v2 on v0

v2 whole, which is shorter than its diff:
```python
import jax
import jax.numpy as jnp
from jax import lax
from jax.experimental import pallas as pl
from jax.experimental.pallas import tpu as pltpu
from jax.sharding import PartitionSpec as P

momentum_coef = 0.9
learning_rate = 0.05
F32 = jnp.float32
I32 = jnp.int32
VMEM = pl.BlockSpec(memory_space=pltpu.VMEM)
SMEM = pl.BlockSpec(memory_space=pltpu.SMEM)
HBM = pl.BlockSpec(memory_space=pltpu.HBM)
DMA = pltpu.SemaphoreType.DMA
EXACT = lax.Precision.HIGHEST
CHUNKS = 8
FRONT = 4
VMEM_ALL = 67_000_000


def cost(nbytes):
    return pl.CostEstimate(flops=0, transcendentals=0, bytes_accessed=nbytes)


def copy(src, dst, sem):
    return pltpu.make_async_copy(src, dst, sem)


def front(sel_ref, grad_ref, res_ref, rows_ref, nr_ref, ids, ids_v, pair, a, b, id_sem, row_sem, in_sem, out_sem):
    cap, owners = ids.shape
    step = grad_ref.shape[0] // CHUNKS
    bound = FRONT * step
    mine = sel_ref.at[pl.ds(lax.axis_index("dp") * cap, cap)]
    ids_copies = copy(mine, ids, id_sem.at[0]), copy(mine, ids_v, id_sem.at[1])
    for c in ids_copies:
        c.start()
    ins = []
    for i in range(FRONT):
        part = pl.ds(i * step, step)
        ins.append((copy(grad_ref.at[part], a.at[part], in_sem.at[0, i]), copy(res_ref.at[part], b.at[part], in_sem.at[1, i])))
        ins[-1][0].start()
        ins[-1][1].start(priority=1)
    for c in ids_copies:
        c.wait()
    top = jnp.max(ids_v[...], axis=0, keepdims=True)
    streamed = jnp.sum((top < bound).astype(F32)).astype(I32)

    def fetch(o, carry):
        theirs = [ids[c, o] for c in range(cap)]
        for c in range(cap):
            block, slot = pl.ds(theirs[c], 1), pl.ds(o * cap + c, 1)
            copy(grad_ref.at[block], pair.at[0, slot], row_sem).start()
            copy(res_ref.at[block], pair.at[1, slot], row_sem).start(priority=1)
        return carry

    lax.fori_loop(streamed, owners, fetch, 0)
    outs = []
    for i in range(FRONT):
        part = pl.ds(i * step, step)
        ins[i][0].wait()
        ins[i][1].wait()
        a[part, :] = a[part, :] + b[part, :]
        outs.append(copy(a.at[part], nr_ref.at[part], out_sem.at[i]))
        outs[-1].start()

    def pick(o, carry):
        theirs = [a[pl.ds(ids[c, o], 1), :] for c in range(cap)]
        for c in range(cap):
            rows_ref[pl.ds(o * cap + c, 1), :] = theirs[c]
        return carry

    lax.fori_loop(0, streamed, pick, 0)

    def land(o, carry):
        four = pl.ds(0, cap)
        copy(grad_ref.at[four], pair.at[0, four], row_sem).wait()
        copy(res_ref.at[four], pair.at[1, four], row_sem).wait()
        return carry

    lax.fori_loop(streamed, owners, land, 0)

    def add(o, carry):
        part = pl.ds(o * cap, cap)
        rows_ref[part, :] = pair[0, part, :] + pair[1, part, :]
        return carry

    lax.fori_loop(streamed, owners, add, 0)
    for c in outs:
        c.wait()


def middle(
    cap,
    sel_ref,
    scount_ref,
    gath_ref,
    gcount_ref,
    grad_ref,
    res_ref,
    nr_in,
    nr_ref,
    hot_ref,
    plan_ref,
    sel_v,
    scount_v,
    plan,
    a,
    b,
    idx_sem,
    in_sem,
    out_sem,
):
    del nr_in
    blocks = grad_ref.shape[0]
    step = blocks // CHUNKS
    base = FRONT * step
    me = lax.axis_index("dp")
    slots, owners = gath_ref.shape
    idx = copy(sel_ref, sel_v, idx_sem.at[0]), copy(scount_ref, scount_v, idx_sem.at[1])
    for c in idx:
        c.start()
    ins = []
    for i in range(CHUNKS - FRONT):
        part, here = pl.ds(base + i * step, step), pl.ds(i * step, step)
        ins.append((copy(grad_ref.at[part], a.at[here], in_sem.at[0, i]), copy(res_ref.at[part], b.at[here], in_sem.at[1, i])))
        ins[-1][0].start()
        ins[-1][1].start(priority=1)
    for c in idx:
        c.wait()

    lane = lax.broadcasted_iota(I32, (slots, owners), 1)
    gath = gath_ref[...]
    gcount = jnp.broadcast_to(gcount_ref[...], (slots, owners))
    listed = lax.broadcasted_iota(I32, (slots, owners), 0) < gcount
    ids = sel_v[pl.ds(me * cap, cap), :]
    count = jnp.broadcast_to(scount_v[pl.ds(me, 1), :], (cap, owners))
    sent = lax.broadcasted_iota(I32, (cap, owners), 0) < count
    hit = jnp.zeros((cap, owners), I32)
    for k in range(slots):
        same = (ids == jnp.broadcast_to(gath_ref[pl.ds(k, 1), :], (cap, owners))) & (gcount[:cap] > k)
        hit = hit + same.astype(I32)
    plan_ref[pl.ds(0, cap), :] = jnp.where(sent & (hit > 0), ids, blocks)
    edge = lax.broadcasted_iota(I32, (CHUNKS, owners), 0) * step
    top = jnp.broadcast_to(jnp.max(gath, axis=0, keepdims=True), (CHUNKS, owners))
    low = jnp.broadcast_to(jnp.min(gath, axis=0, keepdims=True), (CHUNKS, owners))
    first = jnp.sum((top < edge).astype(F32), axis=1, keepdims=True)
    last = jnp.sum((low < edge + step).astype(F32), axis=1, keepdims=True)
    plan_ref[pl.ds(8, CHUNKS), :] = jnp.broadcast_to(first, (CHUNKS, owners)).astype(I32)
    plan_ref[pl.ds(16, CHUNKS), :] = jnp.broadcast_to(last, (CHUNKS, owners)).astype(I32)
    to_smem = copy(plan_ref, plan, idx_sem.at[0])
    to_smem.start()

    mine = jnp.sum(jnp.where((lane == me) & listed, gath + 1, 0).astype(F32), axis=1, keepdims=True) - 1.0
    mine = jnp.where(mine < 0.0, -2.0, mine)
    pick = (lane == me).astype(F32)
    scount = scount_v[...]
    for c in range(cap):
        theirs = jnp.where(scount > c, sel_v[pl.ds(c, owners, stride=cap), :], -1).astype(F32)
        here = lax.dot_general(pick, theirs, (((1,), (1,)), ((), ())), precision=EXACT, preferred_element_type=F32)
        hot_ref[pl.ds(c * slots, slots), :] = (here == mine).astype(F32)
    to_smem.wait()

    zero = jnp.zeros((1, a.shape[1]), F32)
    outs = []
    for i in range(CHUNKS - FRONT):
        part, here = pl.ds(base + i * step, step), pl.ds(i * step, step)
        ins[i][0].wait()
        ins[i][1].wait()
        a[here, :] = a[here, :] + b[here, :]
        lo, hi = base + i * step, base + (i + 1) * step

        def clear(o, carry):
            for block in [plan[c, o] for c in range(cap)]:
                a[pl.ds(jnp.where((block >= lo) & (block < hi), block, blocks) - base, 1), :] = zero
            return carry

        lax.fori_loop(plan[8 + FRONT + i, 0], plan[16 + FRONT + i, 0], clear, 0)
        outs.append(copy(a.at[here], nr_ref.at[part], out_sem.at[i]))
        outs[-1].start()

    for c in outs:
        c.wait()


def reduce_rows(hot_ref, rows_ref, out_ref):
    owners = hot_ref.shape[1]
    cap = rows_ref.shape[0] // owners
    slots = hot_ref.shape[0] // cap
    sums = jnp.zeros((slots, rows_ref.shape[1]), F32)
    for c in range(cap):
        sums = sums + jnp.dot(
            hot_ref[pl.ds(c * slots, slots), :],
            rows_ref[pl.ds(c, owners, stride=cap), :],
            precision=EXACT,
            preferred_element_type=F32,
        )
    out_ref[...] = jnp.broadcast_to(sums[None], (owners,) + sums.shape).reshape(out_ref.shape)


def early(cap, plan, gath, w_ref, m_ref, nr_in, nw_ref, nm_ref, wrow_ref, mrow_ref, nr_ref, zeros, w, m, row_sem, in_sem, out_sem):
    del nr_in
    step = w_ref.shape[0] // CHUNKS
    slots = gath.shape[0]
    ins = []
    for i in range(CHUNKS):
        part = pl.ds(i * step, step)
        ins.append((copy(m_ref.at[part], m.at[part], in_sem.at[0, i]), copy(w_ref.at[part], w.at[part], in_sem.at[1, i])))
        ins[-1][0].start()
        ins[-1][1].start(priority=1)
    zeros[...] = jnp.zeros_like(zeros)

    def wipe(o, issued):
        for block in [plan[c, o] for c in range(cap)]:
            ours = block < FRONT * step

            @pl.when(ours)
            def _():
                copy(zeros.at[pl.ds(0, 1)], nr_ref.at[pl.ds(block, 1)], row_sem).start()

            issued = issued + ours.astype(I32)
        return issued

    issued = lax.fori_loop(0, plan[16 + FRONT - 1, 0], wipe, 0)
    outs = []
    for i in range(CHUNKS):
        part = pl.ds(i * step, step)
        ins[i][0].wait()
        ins[i][1].wait()
        base = momentum_coef * m[part, :]
        m[part, :] = base
        w[part, :] = w[part, :] - learning_rate * base
        outs.append(copy(m.at[part], nm_ref.at[part], out_sem.at[0, i]))
        outs.append(copy(w.at[part], nw_ref.at[part], out_sem.at[1, i]))
        outs[-2].start()
        outs[-1].start()

    def pick(o, carry):
        listed = [pl.ds(gath[k, o], 1) for k in range(slots)]
        mrows = [m[block, :] for block in listed]
        wrows = [w[block, :] for block in listed]
        for k in range(slots):
            slot = pl.ds(o * slots + k, 1)
            mrow_ref[slot, :] = mrows[k]
            wrow_ref[slot, :] = wrows[k]
        return carry

    lax.fori_loop(0, gath.shape[1], pick, 0)

    def land(o, carry):
        copy(zeros.at[pl.ds(0, 1)], nr_ref.at[pl.ds(0, 1)], row_sem).wait()
        return carry

    lax.fori_loop(0, issued, land, 0)
    for c in outs:
        c.wait()


def late(gath, count, u_ref, wrow_ref, mrow_ref, nw_in, nm_in, nw_ref, nm_ref, sums, wrow, mrow, list_sem, row_sem):
    del nw_in, nm_in
    slots, owners = gath.shape
    lists = copy(u_ref, sums, list_sem.at[0]), copy(mrow_ref, mrow, list_sem.at[1]), copy(wrow_ref, wrow, list_sem.at[2])
    for c in lists:
        c.start()
    for c in lists:
        c.wait()

    def patch(o, issued):
        part = pl.ds(pl.multiple_of(o * slots, slots), slots)
        mrow[part, :] = mrow[part, :] + sums[part, :]
        wrow[part, :] = wrow[part, :] - learning_rate * sums[part, :]
        used = count[0, o]
        listed = [gath[k, o] for k in range(slots)]
        for k in range(slots):

            @pl.when(k < used)
            def _():
                slot, block = pl.ds(o * slots + k, 1), pl.ds(listed[k], 1)
                copy(mrow.at[slot], nm_ref.at[block], row_sem.at[0]).start()
                copy(wrow.at[slot], nw_ref.at[block], row_sem.at[1]).start()

        return issued + used

    issued = lax.fori_loop(0, owners, patch, jnp.int32(0))
    size = slots * owners
    while size:
        part = pl.ds(0, size)

        @pl.when((issued & size) != 0)
        def _():
            copy(mrow.at[part], nm_ref.at[part], row_sem.at[0]).wait()
            copy(wrow.at[part], nw_ref.at[part], row_sem.at[1]).wait()

        size //= 2


def local(gradient, residual, weights, momentum, sel_idx, sel_count, gath_idx, gath_count):
    grad, res = gradient[0], residual[0]
    blocks, width = grad.shape
    owners, cap = sel_idx.shape[1:]
    slots = gath_idx.shape[1]
    step = blocks // CHUNKS
    sel = jnp.transpose(sel_idx, (0, 2, 1)).reshape(owners * cap, owners)
    gath = jnp.transpose(gath_idx, (1, 0))
    full = jax.ShapeDtypeStruct((blocks, width), F32)
    listed_rows = jax.ShapeDtypeStruct((owners * slots, width), F32)
    params = pltpu.CompilerParams(vmem_limit_bytes=VMEM_ALL)

    rows, nr = pl.pallas_call(
        front,
        out_shape=(jax.ShapeDtypeStruct((owners * cap, width), F32), full),
        in_specs=[HBM, HBM, HBM],
        out_specs=(VMEM, HBM),
        scratch_shapes=[
            pltpu.SMEM((cap, owners), I32),
            pltpu.VMEM((cap, owners), I32),
            pltpu.VMEM((2, owners * cap, width), F32),
            pltpu.VMEM((FRONT * step, width), F32),
            pltpu.VMEM((FRONT * step, width), F32),
            DMA((2,)),
            DMA(()),
            DMA((2, FRONT)),
            DMA((FRONT,)),
        ],
        compiler_params=params,
        cost_estimate=cost(FRONT * step * width * 12),
        name="front",
    )(sel, grad, res)
    got = lax.all_to_all(rows.reshape(owners, cap, width), "dp", 0, 0, tiled=True)

    rest = (CHUNKS - FRONT) * step
    nr, hot, plan = pl.pallas_call(
        lambda *refs: middle(cap, *refs),
        out_shape=(full, jax.ShapeDtypeStruct((cap * slots, owners), F32), jax.ShapeDtypeStruct((24, owners), I32)),
        in_specs=[HBM, HBM, VMEM, VMEM, HBM, HBM, HBM],
        out_specs=(HBM, VMEM, VMEM),
        scratch_shapes=[
            pltpu.VMEM((owners * cap, owners), I32),
            pltpu.VMEM((owners, owners), I32),
            pltpu.SMEM((24, owners), I32),
            pltpu.VMEM((rest + 8, width), F32),
            pltpu.VMEM((rest, width), F32),
            DMA((2,)),
            DMA((2, CHUNKS - FRONT)),
            DMA((CHUNKS - FRONT,)),
        ],
        input_output_aliases={6: 0},
        compiler_params=params,
        cost_estimate=cost(rest * width * 12),
        name="middle",
    )(sel, sel_count, gath, gath_count.reshape(1, owners), grad, res, nr)

    shared = pl.pallas_call(
        reduce_rows,
        out_shape=listed_rows,
        in_specs=[VMEM, VMEM],
        out_specs=VMEM,
        compiler_params=params,
        cost_estimate=cost(owners * slots * width * 8),
        name="reduce_rows",
    )(hot, got.reshape(owners * cap, width))
    sums = lax.all_to_all(shared.reshape(owners, slots, width), "dp", 0, 0, tiled=True)

    nw, nm, wrow, mrow, new_residual = pl.pallas_call(
        lambda *refs: early(cap, *refs),
        out_shape=(full, full, listed_rows, listed_rows, full),
        in_specs=[SMEM, SMEM, HBM, HBM, HBM],
        out_specs=(HBM, HBM, VMEM, VMEM, HBM),
        scratch_shapes=[
            pltpu.VMEM((8, width), F32),
            pltpu.VMEM((blocks, width), F32),
            pltpu.VMEM((blocks, width), F32),
            DMA(()),
            DMA((2, CHUNKS)),
            DMA((2, CHUNKS)),
        ],
        input_output_aliases={4: 4},
        compiler_params=params,
        cost_estimate=cost(blocks * width * 16),
        name="early",
    )(plan, gath, weights, momentum, nr)

    new_weights, new_momentum = pl.pallas_call(
        late,
        out_shape=(full, full),
        in_specs=[SMEM, SMEM, HBM, HBM, HBM, HBM, HBM],
        out_specs=(HBM, HBM),
        scratch_shapes=[
            pltpu.VMEM((owners * slots, width), F32),
            pltpu.VMEM((owners * slots, width), F32),
            pltpu.VMEM((owners * slots, width), F32),
            DMA((3,)),
            DMA((2,)),
        ],
        input_output_aliases={5: 0, 6: 1},
        compiler_params=params,
        cost_estimate=cost(owners * slots * width * 20),
        name="late",
    )(gath, gath_count.reshape(1, owners), sums.reshape(owners * slots, width), wrow, mrow, nw, nm)
    return new_weights, new_momentum, new_residual[None]


def solution(mesh):
    placed = (P("dp", None, None), P("dp", None, None), P(), P(), P(), P(), P(), P())
    return jax.shard_map(
        local,
        mesh=mesh,
        in_specs=placed,
        out_specs=(P(), P(), P("dp", None, None)),
        check_vma=False,
    )
```

time: 216 us -> 62.1 us (0.29)
  waiting for transfers between devices: 143 us -> 3.62 us
  other arithmetic: 55.9 us -> 0 us
  Pallas kernels: 0 us -> 38.8 us
  starting transfers between devices: 0.04 us -> 18.6 us
  between operations: 14.1 us -> 0.68 us
  local copies, waits for them, and re-layouts: 2.88 us -> 0 us
    psum x1 -> x0, waiting for transfers between devices: 143 us -> none  [local(): summed = lax.psum(accumulated * my_mask[:, None], 'dp')]
    pallas_call x0 -> x5, Pallas kernels: none -> 38.8 us  [the longest x1 14 us: local(): pl.pallas_call(lambda *refs: early(cap, *refs), out_shape=(full, full, li...]
    mul x2 -> x0, other arithmetic: 26.5 us -> none  [the longest x1 13.3 us: local(): summed = lax.psum(accumulated * my_mask[:, None], 'dp')]
    all_to_all x0 -> x2, starting transfers between devices: none -> 18.6 us  [the longest x1 12 us: local(): lax.all_to_all(rows.reshape(owners, cap, width), 'dp', 0, 0, tiled=True)]
    sub x2 -> x0, other arithmetic: 17.8 us -> none  [the longest x1 17.8 us: local(): new_weights = weights - learning_rate * new_momentum]
    another operation x2 -> x0, other arithmetic: 11.5 us -> none  [the longest x1 7.46 us: local(): jnp.zeros((block_count,), jnp.float32).at[gath_idx.reshape(-1)]]
    all_to_all x0 -> x2, waiting for transfers between devices: none -> 3.62 us  [the longest x1 3.62 us: local(): lax.all_to_all(rows.reshape(owners, cap, width), 'dp', 0, 0, tiled=True)]
  transfers between devices with their start and end apart: 1 -> 2, of which waited for: 1 -> 1; matrix products, arithmetic and copies ran while one was open for 10% -> 0% of each run, Pallas kernels for 0% -> 34%
where the time goes in v2:
time: 62.1 us; the launch traced here: 61.6 us
  Pallas kernels  38.8 us (62%)
  starting transfers between devices  18.6 us (30%)
  waiting for transfers between devices  3.62 us (6%)
  between operations  0.68 us (1%)
    pallas_call x1, Pallas kernels, local(): pl.pallas_call(lambda *refs: early(cap, *refs), out_shape=(full, full, li...  14 us
    all_to_all x1, starting transfers between devices, local(): lax.all_to_all(rows.reshape(owners, cap, width), 'dp', 0, 0, tiled=True)  12 us
    pallas_call x1, Pallas kernels, local(): pl.pallas_call(late, out_shape=(full, full), in_specs=[SMEM, SMEM, HBM, H...  9.26 us
    pallas_call x1, Pallas kernels, local(): pl.pallas_call(lambda *refs: middle(cap, *refs), out_shape=(full, jax.Sha...  7.09 us
    all_to_all x1, starting transfers between devices, local(): lax.all_to_all(shared.reshape(owners, slots, width), 'dp', 0, 0, tiled=True)  6.61 us
    pallas_call x1, Pallas kernels, local(): pl.pallas_call(front, out_shape=(jax.ShapeDtypeStruct((owners * cap, widt...  6.27 us
    all_to_all x1, waiting for transfers between devices, local(): lax.all_to_all(rows.reshape(owners, cap, width), 'dp', 0, 0, tiled=True)  3.62 us
    pallas_call x1, Pallas kernels, local(): pl.pallas_call(reduce_rows, out_shape=listed_rows, in_specs=[VMEM, VMEM],...  2.11 us
  transfers between devices with their start and end apart: 2, of which 1 were waited for; matrix products, arithmetic and copies ran while one was open for 0% of the time, Pallas kernels for 34%

profile of v2, /device:TPU:1, one launch (start us, length us, event | category | flops | bytes accessed | tf_op | source)
XLA Modules:
  0.0 61.6 jit_solution(5943610937377915245)
XLA Ops:
  0.6 6.3 %front.1 = (f32[512,128]{1,0:T(8,128)}, f32[16384,128]{1,0:T(8,128)}) custom-call(s32[512,128]{1,0:T(8,128)} %bitcast.18, f32[16384,128]{1,0:T(8,128)} %bitcast.12, f32[16384,128]{1,0:T(8,128)} %bitcast.14), custom_call_target="tpu_custom_call" | custom-call | bytes 12582912 | tf_op jit(solution)/shard_map/front/pallas_call | solution.py:309
  6.9 12.0 %all-to-all-start = ((f32[128,4,128]{2,1,0:T(4,128)}), f32[128,4,128]{2,1,0:T(4,128)}, u32[]{:S(2)}, u32[]{:S(2)}) async-start(f32[128,4,128]{2,1,0:T(4,128)} %bitcast.20), calls=%async_computation | async-start | bytes 524288 | tf_op jit(solution)/shard_map/all_to_all | solution.py:329
  18.9 7.1 %middle.1 = (f32[16384,128]{1,0:T(8,128)}, f32[32,128]{1,0:T(8,128)}, s32[24,128]{1,0:T(8,128)}) custom-call(s32[512,128]{1,0:T(8,128)} %bitcast.19, s32[128,128]{1,0:T(8,128)} %refs_1_.1, s32[8,128]{1,0:T(8,128)} %bitcast.21, s32[1,128]{1,0:T(1,128)} %bitcast.24, f32[16384,128]{1,0:T(8,128)} %bitcast.13, ...), custom_call_target="tpu_custom_call", output_to_operand_aliasing={{0}: (6, {})} | custom-call | bytes 12582912 | tf_op jit(solution)/shard_map/middle/pallas_call | solution.py:332
  26.0 3.6 %all-to-all-done = f32[128,4,128]{2,1,0:T(4,128)} async-done(((f32[128,4,128]{2,1,0:T(4,128)}), f32[128,4,128]{2,1,0:T(4,128)}, u32[]{:S(2)}, u32[]{:S(2)}) %all-to-all-start) | async-done | bytes 262176 | tf_op jit(solution)/shard_map/all_to_all | solution.py:329
  29.6 2.1 %reduce_rows.1 = f32[1024,128]{1,0:T(8,128)} custom-call(f32[32,128]{1,0:T(8,128)} %get-tuple-element.16.hot_ref, f32[512,128]{1,0:T(8,128)} %bitcast.8.rows_ref), custom_call_target="tpu_custom_call" | custom-call | bytes 1048576 | tf_op jit(solution)/shard_map/reduce_rows/pallas_call | solution.py:353
  31.7 6.6 %all-to-all-start.1 = ((f32[128,8,128]{2,1,0:T(8,128)}), f32[128,8,128]{2,1,0:T(8,128)}, u32[]{:S(2)}, u32[]{:S(2)}) async-start(f32[128,8,128]{2,1,0:T(8,128)} %bitcast.17), calls=%async_computation.1 | async-start | bytes 1048576 | tf_op jit(solution)/shard_map/all_to_all | solution.py:362
  38.3 14.0 %early.1 = (f32[16384,128]{1,0:T(8,128)}, f32[16384,128]{1,0:T(8,128)}, f32[1024,128]{1,0:T(8,128)}, f32[1024,128]{1,0:T(8,128)}, f32[16384,128]{1,0:T(8,128)}) custom-call(s32[24,128]{1,0:T(8,128)} %get-tuple-element.18.refs_0_, s32[8,128]{1,0:T(8,128)} %bitcast.22, f32[16384,128]{1,0:T(8,128)} %refs_2_.1, ...), custom_call_target="tpu_custom_call", output_to_operand_aliasing={{4}: (4, {})} | custom-call | bytes 33554432 | tf_op jit(solution)/shard_map/early/pallas_call | solution.py:364
  52.4 0.0 all-to-all-done.1
  52.4 9.3 %late.1 = (f32[16384,128]{1,0:T(8,128)}, f32[16384,128]{1,0:T(8,128)}) custom-call(s32[8,128]{1,0:T(8,128)} %bitcast.23, s32[1,128]{1,0:T(1,128)} %bitcast.25, f32[1024,128]{1,0:T(8,128)} %bitcast.10.u_ref, f32[1024,128]{1,0:T(8,128)} %get-tuple-element.20.wrow_ref, ...), custom_call_target="tpu_custom_call", output_to_operand_aliasing={{0}: (5, {}), {1}: (6, {})} | custom-call | bytes 2621440 | tf_op jit(solution)/shard_map/late/pallas_call | solution.py:383
Async XLA Ops:
  6.9 22.7 %all-to-all-start = ((f32[128,4,128]{2,1,0:T(4,128)}), f32[128,4,128]{2,1,0:T(4,128)}, u32[]{:S(2)}, u32[]{:S(2)}) async-start(f32[128,4,128]{2,1,0:T(4,128)} %bitcast.20), calls=%async_computation | async-start | bytes 524288 | tf_op jit(solution)/shard_map/all_to_all | solution.py:329
  31.7 20.7 %all-to-all-start.1 = ((f32[128,8,128]{2,1,0:T(8,128)}), f32[128,8,128]{2,1,0:T(8,128)}, u32[]{:S(2)}, u32[]{:S(2)}) async-start(f32[128,8,128]{2,1,0:T(8,128)} %bitcast.17), calls=%async_computation.1 | async-start | bytes 1048576 | tf_op jit(solution)/shard_map/all_to_all | solution.py:362

commit v3 on v2

v3 whole, which is shorter than its diff:
```python
import jax
import jax.numpy as jnp
from jax import lax
from jax.experimental import pallas as pl
from jax.experimental.pallas import tpu as pltpu
from jax.sharding import PartitionSpec as P

momentum_coef = 0.9
learning_rate = 0.05
F32 = jnp.float32
I32 = jnp.int32
VMEM = pl.BlockSpec(memory_space=pltpu.VMEM)
HBM = pl.BlockSpec(memory_space=pltpu.HBM)
DMA = pltpu.SemaphoreType.DMA
EXACT = lax.Precision.HIGHEST
CHUNKS = 8
VMEM_ALL = 67_000_000


def cost(nbytes):
    return pl.CostEstimate(flops=0, transcendentals=0, bytes_accessed=nbytes)


def copy(src, dst, sem):
    return pltpu.make_async_copy(src, dst, sem)


def front(sel_ref, grad_ref, res_ref, rows_ref, ids, pair, id_sem, row_sem):
    cap, owners = ids.shape
    mine = copy(sel_ref.at[pl.ds(lax.axis_index("dp") * cap, cap)], ids, id_sem)
    mine.start()
    mine.wait()

    def fetch(o, carry):
        theirs = [ids[c, o] for c in range(cap)]
        for c in range(cap):
            block, slot = pl.ds(theirs[c], 1), pl.ds(o * cap + c, 1)
            copy(grad_ref.at[block], pair.at[0, slot], row_sem.at[0]).start()
            copy(res_ref.at[block], pair.at[1, slot], row_sem.at[1]).start(priority=1)
        return carry

    lax.fori_loop(0, owners, fetch, 0, unroll=2)
    every = pl.ds(0, cap * owners)
    copy(grad_ref.at[every], pair.at[0], row_sem.at[0]).wait()
    copy(res_ref.at[every], pair.at[1], row_sem.at[1]).wait()
    rows_ref[...] = pair[0] + pair[1]


def middle(
    cap,
    sel_ref,
    scount_ref,
    gath_hbm,
    gcount_hbm,
    grad_ref,
    res_ref,
    nr_ref,
    hot_hbm,
    plan_hbm,
    sel_v,
    scount_v,
    gath_ref,
    gcount_ref,
    hot_ref,
    plan_ref,
    plan,
    a,
    b,
    idx_sem,
    in_sem,
    out_sem,
):
    blocks = grad_ref.shape[0]
    step = blocks // CHUNKS
    me = lax.axis_index("dp")
    slots, owners = gath_ref.shape
    idx = (
        copy(gath_hbm, gath_ref, idx_sem.at[2]),
        copy(gcount_hbm, gcount_ref, idx_sem.at[3]),
        copy(scount_ref, scount_v, idx_sem.at[1]),
        copy(sel_ref, sel_v, idx_sem.at[0]),
    )
    for c in idx:
        c.start()
    ins = []
    for i in range(CHUNKS):
        part = pl.ds(i * step, step)
        ins.append((copy(grad_ref.at[part], a.at[part], in_sem.at[0, i]), copy(res_ref.at[part], b.at[part], in_sem.at[1, i])))
        ins[-1][0].start()
        ins[-1][1].start(priority=1)
    for c in idx:
        c.wait()

    lane = lax.broadcasted_iota(I32, (slots, owners), 1)
    gath = gath_ref[...]
    gcount = jnp.broadcast_to(gcount_ref[...], (slots, owners))
    listed = lax.broadcasted_iota(I32, (slots, owners), 0) < gcount
    ids = sel_v[pl.ds(me * cap, cap), :]
    count = jnp.broadcast_to(scount_v[pl.ds(me, 1), :], (cap, owners))
    sent = lax.broadcasted_iota(I32, (cap, owners), 0) < count
    hit = jnp.zeros((cap, owners), I32)
    for k in range(slots):
        same = (ids == jnp.broadcast_to(gath_ref[pl.ds(k, 1), :], (cap, owners))) & (gcount[:cap] > k)
        hit = hit + same.astype(I32)
    plan_ref[pl.ds(0, cap), :] = jnp.where(sent & (hit > 0), ids, blocks)
    edge = lax.broadcasted_iota(I32, (CHUNKS, owners), 0) * step
    top = jnp.broadcast_to(jnp.max(gath, axis=0, keepdims=True), (CHUNKS, owners))
    low = jnp.broadcast_to(jnp.min(gath, axis=0, keepdims=True), (CHUNKS, owners))
    first = jnp.sum((top < edge).astype(F32), axis=1, keepdims=True)
    last = jnp.sum((low < edge + step).astype(F32), axis=1, keepdims=True)
    plan_ref[pl.ds(8, CHUNKS), :] = jnp.broadcast_to(first, (CHUNKS, owners)).astype(I32)
    plan_ref[pl.ds(16, CHUNKS), :] = jnp.broadcast_to(last, (CHUNKS, owners)).astype(I32)
    to_smem = copy(plan_ref, plan, idx_sem.at[0])
    to_smem.start()

    mine = jnp.sum(jnp.where((lane == me) & listed, gath + 1, 0).astype(F32), axis=1, keepdims=True) - 1.0
    mine = jnp.where(mine < 0.0, -2.0, mine)
    pick = (lane == me).astype(F32)
    scount = scount_v[...]
    for c in range(cap):
        theirs = jnp.where(scount > c, sel_v[pl.ds(c, owners, stride=cap), :], -1).astype(F32)
        here = lax.dot_general(pick, theirs, (((1,), (1,)), ((), ())), precision=EXACT, preferred_element_type=F32)
        hot_ref[pl.ds(c * slots, slots), :] = (here == mine).astype(F32)
    to_smem.wait()
    outs = [copy(hot_ref, hot_hbm, idx_sem.at[2]), copy(plan_ref, plan_hbm, idx_sem.at[3])]
    for c in outs:
        c.start()
    zero = jnp.zeros((1, a.shape[1]), F32)
    for i in range(CHUNKS):
        part = pl.ds(i * step, step)
        ins[i][0].wait()
        ins[i][1].wait()
        a[part, :] = a[part, :] + b[part, :]
        lo, hi = i * step, (i + 1) * step

        def clear(o, carry):
            for block in [plan[c, o] for c in range(cap)]:
                a[pl.ds(jnp.where((block >= lo) & (block < hi), block, blocks), 1), :] = zero
            return carry

        lax.fori_loop(plan[8 + i, 0], plan[16 + i, 0], clear, 0)
        outs.append(copy(a.at[part], nr_ref.at[part], out_sem.at[i]))
        outs[-1].start()

    for c in outs:
        c.wait()


def reduce_rows(hot_ref, rows_ref, out_ref):
    owners = hot_ref.shape[1]
    cap = rows_ref.shape[0] // owners
    slots = hot_ref.shape[0] // cap
    sums = jnp.zeros((slots, rows_ref.shape[1]), F32)
    for c in range(cap):
        sums = sums + jnp.dot(
            hot_ref[pl.ds(c * slots, slots), :],
            rows_ref[pl.ds(c, owners, stride=cap), :],
            precision=EXACT,
            preferred_element_type=F32,
        )
    out_ref[...] = jnp.broadcast_to(sums[None], (owners,) + sums.shape).reshape(out_ref.shape)


def early(gath_ref, plan_ref, w_ref, m_ref, nw_ref, nm_ref, wrow_ref, mrow_ref, gath, plan, wrow, mrow, w, m, idx_sem, in_sem, out_sem):
    step = w_ref.shape[0] // CHUNKS
    slots, owners = gath.shape
    idx = copy(gath_ref, gath, idx_sem.at[0]), copy(plan_ref, plan, idx_sem.at[1])
    for c in idx:
        c.start()
    ins = []
    for i in range(CHUNKS):
        part = pl.ds(i * step, step)
        ins.append((copy(m_ref.at[part], m.at[part], in_sem.at[0, i]), copy(w_ref.at[part], w.at[part], in_sem.at[1, i])))
        ins[-1][0].start()
        ins[-1][1].start(priority=1)
    for c in idx:
        c.wait()

    def pick(o, carry):
        listed = [pl.ds(gath[k, o], 1) for k in range(slots)]
        mrows = [m[block, :] for block in listed]
        wrows = [w[block, :] for block in listed]
        for k in range(slots):
            slot = pl.ds(o * slots + k, 1)
            mrow[slot, :] = mrows[k]
            wrow[slot, :] = wrows[k]
        return carry

    outs = []
    done = 0
    for i in range(CHUNKS):
        part = pl.ds(i * step, step)
        ins[i][0].wait()
        ins[i][1].wait()
        base = momentum_coef * m[part, :]
        m[part, :] = base
        w[part, :] = w[part, :] - learning_rate * base
        outs.append(copy(m.at[part], nm_ref.at[part], out_sem.at[0, i]))
        outs.append(copy(w.at[part], nw_ref.at[part], out_sem.at[1, i]))
        outs[-2].start()
        outs[-1].start()
        below = plan[8 + i + 1, 0] if i + 1 < CHUNKS else owners
        lax.fori_loop(done, below, pick, 0)
        done = below
    outs.append(copy(mrow, mrow_ref, idx_sem.at[0]))
    outs.append(copy(wrow, wrow_ref, idx_sem.at[1]))
    outs[-2].start()
    outs[-1].start()
    for c in outs:
        c.wait()


def late(gath_ref, count_ref, u_ref, wrow_ref, mrow_ref, nw_in, nm_in, nw_ref, nm_ref, gath, count, sums, wrow, mrow, list_sem, row_sem):
    del nw_in, nm_in
    slots, owners = gath.shape
    lists = (
        copy(gath_ref, gath, list_sem.at[3]),
        copy(count_ref, count, list_sem.at[4]),
        copy(u_ref, sums, list_sem.at[0]),
        copy(mrow_ref, mrow, list_sem.at[1]),
        copy(wrow_ref, wrow, list_sem.at[2]),
    )
    for c, thread in zip(lists, (0, 1, 0, 1, 0)):
        c.start(priority=thread)
    for c in lists:
        c.wait()

    def patch(o, issued):
        part = pl.ds(pl.multiple_of(o * slots, slots), slots)
        mrow[part, :] = mrow[part, :] + sums[part, :]
        wrow[part, :] = wrow[part, :] - learning_rate * sums[part, :]
        used = count[0, o]
        listed = [gath[k, o] for k in range(slots)]
        for k in range(slots):

            @pl.when(k < used)
            def _():
                slot, block = pl.ds(o * slots + k, 1), pl.ds(listed[k], 1)
                copy(mrow.at[slot], nm_ref.at[block], row_sem.at[0]).start()
                copy(wrow.at[slot], nw_ref.at[block], row_sem.at[1]).start(priority=1)

        return issued + used

    issued = lax.fori_loop(0, owners, patch, jnp.int32(0))
    size = slots * owners
    while size:
        part = pl.ds(0, size)

        @pl.when((issued & size) != 0)
        def _():
            copy(mrow.at[part], nm_ref.at[part], row_sem.at[0]).wait()
            copy(wrow.at[part], nw_ref.at[part], row_sem.at[1]).wait()

        size //= 2


def local(gradient, residual, weights, momentum, sel_idx, sel_count, gath_idx, gath_count):
    grad, res = gradient[0], residual[0]
    blocks, width = grad.shape
    owners, cap = sel_idx.shape[1:]
    slots = gath_idx.shape[1]
    sel = jnp.transpose(sel_idx, (0, 2, 1)).reshape(owners * cap, owners)
    gath = jnp.transpose(gath_idx, (1, 0))
    full = jax.ShapeDtypeStruct((blocks, width), F32)
    listed_rows = jax.ShapeDtypeStruct((owners * slots, width), F32)
    params = pltpu.CompilerParams(vmem_limit_bytes=VMEM_ALL)

    rows = pl.pallas_call(
        front,
        out_shape=jax.ShapeDtypeStruct((owners * cap, width), F32),
        in_specs=[HBM, HBM, HBM],
        out_specs=VMEM,
        scratch_shapes=[
            pltpu.SMEM((cap, owners), I32),
            pltpu.VMEM((2, owners * cap, width), F32),
            DMA(()),
            DMA((2,)),
        ],
        compiler_params=params,
        cost_estimate=cost(owners * cap * width * 12),
        name="front",
    )(sel, grad, res)
    got = lax.all_to_all(rows.reshape(owners, cap, width), "dp", 0, 0, tiled=True)

    new_residual, hot, plan = pl.pallas_call(
        lambda *refs: middle(cap, *refs),
        out_shape=(full, jax.ShapeDtypeStruct((cap * slots, owners), F32), jax.ShapeDtypeStruct((24, owners), I32)),
        in_specs=[HBM] * 6,
        out_specs=(HBM, HBM, HBM),
        scratch_shapes=[
            pltpu.VMEM((owners * cap, owners), I32),
            pltpu.VMEM((owners, owners), I32),
            pltpu.VMEM((slots, owners), I32),
            pltpu.VMEM((1, owners), I32),
            pltpu.VMEM((cap * slots, owners), F32),
            pltpu.VMEM((24, owners), I32),
            pltpu.SMEM((24, owners), I32),
            pltpu.VMEM((blocks + 8, width), F32),
            pltpu.VMEM((blocks, width), F32),
            DMA((4,)),
            DMA((2, CHUNKS)),
            DMA((CHUNKS,)),
        ],
        compiler_params=pltpu.CompilerParams(vmem_limit_bytes=60_000_000),
        cost_estimate=cost(blocks * width * 12),
        name="middle",
    )(sel, sel_count, gath, gath_count.reshape(1, owners), grad, res)

    shared = pl.pallas_call(
        reduce_rows,
        out_shape=listed_rows,
        in_specs=[VMEM, VMEM],
        out_specs=VMEM,
        compiler_params=pltpu.CompilerParams(vmem_limit_bytes=8 << 20),
        cost_estimate=cost(owners * slots * width * 8),
        name="reduce_rows",
    )(hot, got.reshape(owners * cap, width))
    sums = lax.all_to_all(shared.reshape(owners, slots, width), "dp", 0, 0, tiled=True)

    nw, nm, wrow, mrow = pl.pallas_call(
        early,
        out_shape=(full, full, listed_rows, listed_rows),
        in_specs=[HBM] * 4,
        out_specs=(HBM,) * 4,
        scratch_shapes=[
            pltpu.SMEM((slots, owners), I32),
            pltpu.SMEM((24, owners), I32),
            pltpu.VMEM((owners * slots, width), F32),
            pltpu.VMEM((owners * slots, width), F32),
            pltpu.VMEM((blocks, width), F32),
            pltpu.VMEM((blocks, width), F32),
            DMA((2,)),
            DMA((2, CHUNKS)),
            DMA((2, CHUNKS)),
        ],
        compiler_params=params,
        cost_estimate=cost(blocks * width * 16),
        name="early",
    )(gath, plan, weights, momentum)

    new_weights, new_momentum = pl.pallas_call(
        late,
        out_shape=(full, full),
        in_specs=[HBM] * 7,
        out_specs=(HBM, HBM),
        scratch_shapes=[
            pltpu.SMEM((slots, owners), I32),
            pltpu.SMEM((1, owners), I32),
            pltpu.VMEM((owners * slots, width), F32),
            pltpu.VMEM((owners * slots, width), F32),
            pltpu.VMEM((owners * slots, width), F32),
            DMA((5,)),
            DMA((2,)),
        ],
        input_output_aliases={5: 0, 6: 1},
        compiler_params=params,
        cost_estimate=cost(owners * slots * width * 20),
        name="late",
    )(gath, gath_count.reshape(1, owners), sums.reshape(owners * slots, width), wrow, mrow, nw, nm)
    return new_weights, new_momentum, new_residual[None]


def solution(mesh):
    placed = (P("dp", None, None), P("dp", None, None), P(), P(), P(), P(), P(), P())
    return jax.shard_map(
        local,
        mesh=mesh,
        in_specs=placed,
        out_specs=(P(), P(), P("dp", None, None)),
        check_vma=False,
    )
```

time: 62.1 us -> 59.2 us (0.953)
  Pallas kernels: 38.8 us -> 33.5 us
  waiting for transfers between devices: 3.62 us -> 4.87 us
  local copies, waits for them, and re-layouts: 0 us -> 0.72 us
    pallas_call x3, Pallas kernels: 29.6 us -> 23.9 us  [the longest x1 11 us: local(): pl.pallas_call(early, out_shape=(full, full, listed_rows, listed_rows), i...]
    all_to_all x1, waiting for transfers between devices: 0.01 us -> 2.27 us  [local(): lax.all_to_all(shared.reshape(owners, slots, width), 'dp', 0, 0, tiled=True)]
    pallas_call x1, Pallas kernels: 7.09 us -> 8.46 us  [local(): pl.pallas_call(lambda *refs: middle(cap, *refs), out_shape=(full, jax.Sha...]
    all_to_all x1, starting transfers between devices: 6.61 us -> 7.63 us  [local(): lax.all_to_all(shared.reshape(owners, slots, width), 'dp', 0, 0, tiled=True)]
    all_to_all x1, waiting for transfers between devices: 3.62 us -> 2.6 us  [local(): lax.all_to_all(rows.reshape(owners, cap, width), 'dp', 0, 0, tiled=True)]
    pallas_call x1, Pallas kernels: 2.11 us -> 1.14 us  [local(): pl.pallas_call(reduce_rows, out_shape=listed_rows, in_specs=[VMEM, VMEM],...]
    unnamed x0 -> x2, local copies, waits for them, and re-layouts: none -> 0.72 us
  transfers between devices with their start and end apart: 2 -> 2, of which waited for: 1 -> 2; matrix products, arithmetic and copies ran while one was open for 0% -> 0% of each run, Pallas kernels for 34% -> 33%
where the time goes in v3:
time: 59.2 us; the launch traced here: 58.9 us
  Pallas kernels  33.5 us (57%)
  starting transfers between devices  19.1 us (32%)
  waiting for transfers between devices  4.87 us (8%)
  local copies, waits for them, and re-layouts  0.72 us (1%)
  between operations  0.67 us (1%)
    all_to_all x1, starting transfers between devices, local(): lax.all_to_all(rows.reshape(owners, cap, width), 'dp', 0, 0, tiled=True)  11.5 us
    pallas_call x1, Pallas kernels, local(): pl.pallas_call(early, out_shape=(full, full, listed_rows, listed_rows), i...  11 us
    pallas_call x1, Pallas kernels, local(): pl.pallas_call(late, out_shape=(full, full), in_specs=[HBM] * 7, out_spec...  8.51 us
    pallas_call x1, Pallas kernels, local(): pl.pallas_call(lambda *refs: middle(cap, *refs), out_shape=(full, jax.Sha...  8.46 us
    all_to_all x1, starting transfers between devices, local(): lax.all_to_all(shared.reshape(owners, slots, width), 'dp', 0, 0, tiled=True)  7.63 us
    pallas_call x1, Pallas kernels, local(): pl.pallas_call(front, out_shape=jax.ShapeDtypeStruct((owners * cap, width...  4.41 us
    all_to_all x1, waiting for transfers between devices, local(): lax.all_to_all(rows.reshape(owners, cap, width), 'dp', 0, 0, tiled=True)  2.6 us
    all_to_all x1, waiting for transfers between devices, local(): lax.all_to_all(shared.reshape(owners, slots, width), 'dp', 0, 0, tiled=True)  2.27 us
  transfers between devices with their start and end apart: 2, of which 2 were waited for; matrix products, arithmetic and copies ran while one was open for 0% of the time, Pallas kernels for 33%

profile of v3, /device:TPU:1, one launch (start us, length us, event | category | flops | bytes accessed | tf_op | source)
XLA Modules:
  0.0 58.9 jit_solution(16450778318005280170)
XLA Ops:
  0.6 4.4 %front.1 = f32[512,128]{1,0:T(8,128)} custom-call(s32[512,128]{1,0:T(8,128)} %bitcast.17, f32[16384,128]{1,0:T(8,128)} %bitcast.13, f32[16384,128]{1,0:T(8,128)} %bitcast.15), custom_call_target="tpu_custom_call" | custom-call | bytes 786432 | tf_op jit(solution)/shard_map/front/pallas_call | solution.py:268
  5.0 11.5 %all-to-all-start = ((f32[128,4,128]{2,1,0:T(4,128)}), f32[128,4,128]{2,1,0:T(4,128)S(1)}, u32[]{:S(2)}, u32[]{:S(2)}) async-start(f32[128,4,128]{2,1,0:T(4,128)} %bitcast.19), calls=%async_computation | async-start | bytes 524288 | tf_op jit(solution)/shard_map/all_to_all | solution.py:283
  16.5 8.5 %middle.1 = (f32[16384,128]{1,0:T(8,128)}, f32[32,128]{1,0:T(8,128)}, s32[24,128]{1,0:T(8,128)}) custom-call(s32[512,128]{1,0:T(8,128)} %bitcast.18, s32[128,128]{1,0:T(8,128)} %refs_1_.1, s32[8,128]{1,0:T(8,128)} %bitcast.20, s32[1,128]{1,0:T(1,128)} %bitcast.23, f32[16384,128]{1,0:T(8,128)} %bitcast.14, f32[16384,128]{1,0:T(8,128)} %bitcast.16), custom_call_target="tpu_custom_call" | custom-call | bytes 25165824 | tf_op jit(solution)/shard_map/middle/pallas_call | solution.py:285
  25.0 2.6 %all-to-all-done = f32[128,4,128]{2,1,0:T(4,128)S(1)} async-done(((f32[128,4,128]{2,1,0:T(4,128)}), f32[128,4,128]{2,1,0:T(4,128)S(1)}, u32[]{:S(2)}, u32[]{:S(2)}) %all-to-all-start) | async-done | bytes 262176 | tf_op jit(solution)/shard_map/all_to_all | solution.py:283
  27.6 0.0 copy-start
  27.6 0.7 %copy-done = f32[32,128]{1,0:T(8,128)S(1)} copy-done((f32[32,128]{1,0:T(8,128)S(1)}, f32[32,128]{1,0:T(8,128)}, u32[]{:S(2)}) %copy-start) | copy-done | bytes 16408
  28.3 1.1 %reduce_rows.1 = f32[1024,128]{1,0:T(8,128)} custom-call(f32[32,128]{1,0:T(8,128)S(1)} %copy-done, f32[512,128]{1,0:T(8,128)S(1)} %bitcast.12), custom_call_target="tpu_custom_call" | custom-call | bytes 1048576 | tf_op jit(solution)/shard_map/reduce_rows/pallas_call | solution.py:309
  29.5 7.6 %all-to-all-start.1 = ((f32[128,8,128]{2,1,0:T(8,128)}), f32[128,8,128]{2,1,0:T(8,128)}, u32[]{:S(2)}, u32[]{:S(2)}) async-start(f32[128,8,128]{2,1,0:T(8,128)} %bitcast.9), calls=%async_computation.1 | async-start | bytes 1048576 | tf_op jit(solution)/shard_map/all_to_all | solution.py:318
  37.1 11.0 %early.1 = (f32[16384,128]{1,0:T(8,128)}, f32[16384,128]{1,0:T(8,128)}, f32[1024,128]{1,0:T(8,128)}, f32[1024,128]{1,0:T(8,128)}) custom-call(s32[8,128]{1,0:T(8,128)} %bitcast.21, s32[24,128]{1,0:T(8,128)} %get-tuple-element.13.plan_ref, f32[16384,128]{1,0:T(8,128)} %w_ref.1, f32[16384,128]{1,0:T(8,128)} %m_ref.1), custom_call_target="tpu_custom_call" | custom-call | bytes 33554432 | tf_op jit(solution)/shard_map/early/pallas_call | solution.py:320
  48.1 2.3 %all-to-all-done.1 = f32[128,8,128]{2,1,0:T(8,128)} async-done(((f32[128,8,128]{2,1,0:T(8,128)}), f32[128,8,128]{2,1,0:T(8,128)}, u32[]{:S(2)}, u32[]{:S(2)}) %all-to-all-start.1) | async-done | bytes 524320 | tf_op jit(solution)/shard_map/all_to_all | solution.py:318
  50.4 8.5 %late.1 = (f32[16384,128]{1,0:T(8,128)}, f32[16384,128]{1,0:T(8,128)}) custom-call(s32[8,128]{1,0:T(8,128)} %bitcast.22, s32[1,128]{1,0:T(1,128)} %bitcast.24, f32[1024,128]{1,0:T(8,128)} %bitcast.10.u_ref, f32[1024,128]{1,0:T(8,128)} %get-tuple-element.14.wrow_ref, ...), custom_call_target="tpu_custom_call", output_to_operand_aliasing={{0}: (5, {}), {1}: (6, {})} | custom-call | bytes 2621440 | tf_op jit(solution)/shard_map/late/pallas_call | solution.py:341
Async XLA Ops:
  5.0 22.6 %all-to-all-start = ((f32[128,4,128]{2,1,0:T(4,128)}), f32[128,4,128]{2,1,0:T(4,128)S(1)}, u32[]{:S(2)}, u32[]{:S(2)}) async-start(f32[128,4,128]{2,1,0:T(4,128)} %bitcast.19), calls=%async_computation | async-start | bytes 524288 | tf_op jit(solution)/shard_map/all_to_all | solution.py:283
  27.6 0.7 %copy-start = (f32[32,128]{1,0:T(8,128)S(1)}, f32[32,128]{1,0:T(8,128)}, u32[]{:S(2)}) copy-start(f32[32,128]{1,0:T(8,128)} %get-tuple-element.12.hot_ref) | copy-start | bytes 49156
  29.5 20.9 %all-to-all-start.1 = ((f32[128,8,128]{2,1,0:T(8,128)}), f32[128,8,128]{2,1,0:T(8,128)}, u32[]{:S(2)}, u32[]{:S(2)}) async-start(f32[128,8,128]{2,1,0:T(8,128)} %bitcast.9), calls=%async_computation.1 | async-start | bytes 1048576 | tf_op jit(solution)/shard_map/all_to_all | solution.py:318

commit v4 on v3

--- a/solution.py
+++ b/solution.py
@@ -213,15 +213,15 @@
 def late(gath_ref, count_ref, u_ref, wrow_ref, mrow_ref, nw_in, nm_in, nw_ref, nm_ref, gath, count, sums, wrow, mrow, list_sem, row_sem):
     del nw_in, nm_in
     slots, owners = gath.shape
-    lists = (
-        copy(gath_ref, gath, list_sem.at[3]),
-        copy(count_ref, count, list_sem.at[4]),
-        copy(u_ref, sums, list_sem.at[0]),
-        copy(mrow_ref, mrow, list_sem.at[1]),
-        copy(wrow_ref, wrow, list_sem.at[2]),
-    )
-    for c, thread in zip(lists, (0, 1, 0, 1, 0)):
-        c.start(priority=thread)
+    half = owners // 2
+    lists = [copy(gath_ref, gath, list_sem.at[0, 3]), copy(count_ref, count, list_sem.at[0, 4])]
+    later = []
+    for i, group in enumerate((lists, later)):
+        part = pl.ds(i * half * slots, half * slots)
+        for j, (src, dst) in enumerate(((u_ref, sums), (mrow_ref, mrow), (wrow_ref, wrow))):
+            group.append(copy(src.at[part], dst.at[part], list_sem.at[i, j]))
+    for j, c in enumerate(lists + later):
+        c.start(priority=j % 2)
     for c in lists:
         c.wait()
 
@@ -241,7 +241,10 @@
 
         return issued + used
 
-    issued = lax.fori_loop(0, owners, patch, jnp.int32(0))
+    issued = lax.fori_loop(0, half, patch, jnp.int32(0))
+    for c in later:
+        c.wait()
+    issued = lax.fori_loop(half, owners, patch, issued)
     size = slots * owners
     while size:
         part = pl.ds(0, size)
@@ -349,7 +352,7 @@
             pltpu.VMEM((owners * slots, width), F32),
             pltpu.VMEM((owners * slots, width), F32),
             pltpu.VMEM((owners * slots, width), F32),
-            DMA((5,)),
+            DMA((2, 5)),
             DMA((2,)),
         ],
         input_output_aliases={5: 0, 6: 1},

time: 59.2 us -> 59.2 us (level)
  no operation moved by 1% of the time
where the time goes in v4:
time: 59.2 us; the launch traced here: 58.9 us
  Pallas kernels  33.5 us (57%)
  starting transfers between devices  19.1 us (32%)
  waiting for transfers between devices  4.89 us (8%)
  local copies, waits for them, and re-layouts  0.72 us (1%)
  between operations  0.67 us (1%)
    all_to_all x1, starting transfers between devices, local(): lax.all_to_all(rows.reshape(owners, cap, width), 'dp', 0, 0, tiled=True)  11.5 us
    pallas_call x1, Pallas kernels, local(): pl.pallas_call(early, out_shape=(full, full, listed_rows, listed_rows), i...  11 us
    pallas_call x1, Pallas kernels, local(): pl.pallas_call(late, out_shape=(full, full), in_specs=[HBM] * 7, out_spec...  8.55 us
    pallas_call x1, Pallas kernels, local(): pl.pallas_call(lambda *refs: middle(cap, *refs), out_shape=(full, jax.Sha...  8.44 us
    all_to_all x1, starting transfers between devices, local(): lax.all_to_all(shared.reshape(owners, slots, width), 'dp', 0, 0, tiled=True)  7.61 us
    pallas_call x1, Pallas kernels, local(): pl.pallas_call(front, out_shape=jax.ShapeDtypeStruct((owners * cap, width...  4.41 us
    all_to_all x1, waiting for transfers between devices, local(): lax.all_to_all(rows.reshape(owners, cap, width), 'dp', 0, 0, tiled=True)  2.62 us
    all_to_all x1, waiting for transfers between devices, local(): lax.all_to_all(shared.reshape(owners, slots, width), 'dp', 0, 0, tiled=True)  2.27 us
  transfers between devices with their start and end apart: 2, of which 2 were waited for; matrix products, arithmetic and copies ran while one was open for 0% of the time, Pallas kernels for 33%

profile of v4, /device:TPU:1, one launch (start us, length us, event | category | flops | bytes accessed | tf_op | source)
XLA Modules:
  0.0 58.9 jit_solution(16035430305167574128)
XLA Ops:
  0.6 4.4 %front.1 = f32[512,128]{1,0:T(8,128)} custom-call(s32[512,128]{1,0:T(8,128)} %bitcast.17, f32[16384,128]{1,0:T(8,128)} %bitcast.13, f32[16384,128]{1,0:T(8,128)} %bitcast.15), custom_call_target="tpu_custom_call" | custom-call | bytes 786432 | tf_op jit(solution)/shard_map/front/pallas_call | solution.py:271
  5.0 11.5 %all-to-all-start = ((f32[128,4,128]{2,1,0:T(4,128)}), f32[128,4,128]{2,1,0:T(4,128)S(1)}, u32[]{:S(2)}, u32[]{:S(2)}) async-start(f32[128,4,128]{2,1,0:T(4,128)} %bitcast.19), calls=%async_computation | async-start | bytes 524288 | tf_op jit(solution)/shard_map/all_to_all | solution.py:286
  16.5 8.4 %middle.1 = (f32[16384,128]{1,0:T(8,128)}, f32[32,128]{1,0:T(8,128)}, s32[24,128]{1,0:T(8,128)}) custom-call(s32[512,128]{1,0:T(8,128)} %bitcast.18, s32[128,128]{1,0:T(8,128)} %refs_1_.1, s32[8,128]{1,0:T(8,128)} %bitcast.20, s32[1,128]{1,0:T(1,128)} %bitcast.23, f32[16384,128]{1,0:T(8,128)} %bitcast.14, f32[16384,128]{1,0:T(8,128)} %bitcast.16), custom_call_target="tpu_custom_call" | custom-call | bytes 25165824 | tf_op jit(solution)/shard_map/middle/pallas_call | solution.py:288
  25.0 2.6 %all-to-all-done = f32[128,4,128]{2,1,0:T(4,128)S(1)} async-done(((f32[128,4,128]{2,1,0:T(4,128)}), f32[128,4,128]{2,1,0:T(4,128)S(1)}, u32[]{:S(2)}, u32[]{:S(2)}) %all-to-all-start) | async-done | bytes 262176 | tf_op jit(solution)/shard_map/all_to_all | solution.py:286
  27.6 0.0 copy-start
  27.6 0.7 %copy-done = f32[32,128]{1,0:T(8,128)S(1)} copy-done((f32[32,128]{1,0:T(8,128)S(1)}, f32[32,128]{1,0:T(8,128)}, u32[]{:S(2)}) %copy-start) | copy-done | bytes 16408
  28.3 1.1 %reduce_rows.1 = f32[1024,128]{1,0:T(8,128)} custom-call(f32[32,128]{1,0:T(8,128)S(1)} %copy-done, f32[512,128]{1,0:T(8,128)S(1)} %bitcast.12), custom_call_target="tpu_custom_call" | custom-call | bytes 1048576 | tf_op jit(solution)/shard_map/reduce_rows/pallas_call | solution.py:312
  29.5 7.6 %all-to-all-start.1 = ((f32[128,8,128]{2,1,0:T(8,128)}), f32[128,8,128]{2,1,0:T(8,128)}, u32[]{:S(2)}, u32[]{:S(2)}) async-start(f32[128,8,128]{2,1,0:T(8,128)} %bitcast.9), calls=%async_computation.1 | async-start | bytes 1048576 | tf_op jit(solution)/shard_map/all_to_all | solution.py:321
  37.1 11.0 %early.1 = (f32[16384,128]{1,0:T(8,128)}, f32[16384,128]{1,0:T(8,128)}, f32[1024,128]{1,0:T(8,128)}, f32[1024,128]{1,0:T(8,128)}) custom-call(s32[8,128]{1,0:T(8,128)} %bitcast.21, s32[24,128]{1,0:T(8,128)} %get-tuple-element.13.plan_ref, f32[16384,128]{1,0:T(8,128)} %w_ref.1, f32[16384,128]{1,0:T(8,128)} %m_ref.1), custom_call_target="tpu_custom_call" | custom-call | bytes 33554432 | tf_op jit(solution)/shard_map/early/pallas_call | solution.py:323
  48.1 2.3 %all-to-all-done.1 = f32[128,8,128]{2,1,0:T(8,128)} async-done(((f32[128,8,128]{2,1,0:T(8,128)}), f32[128,8,128]{2,1,0:T(8,128)}, u32[]{:S(2)}, u32[]{:S(2)}) %all-to-all-start.1) | async-done | bytes 524320 | tf_op jit(solution)/shard_map/all_to_all | solution.py:321
  50.4 8.6 %late.1 = (f32[16384,128]{1,0:T(8,128)}, f32[16384,128]{1,0:T(8,128)}) custom-call(s32[8,128]{1,0:T(8,128)} %bitcast.22, s32[1,128]{1,0:T(1,128)} %bitcast.24, f32[1024,128]{1,0:T(8,128)} %bitcast.10.u_ref, f32[1024,128]{1,0:T(8,128)} %get-tuple-element.14.wrow_ref, ...), custom_call_target="tpu_custom_call", output_to_operand_aliasing={{0}: (5, {}), {1}: (6, {})} | custom-call | bytes 2621440 | tf_op jit(solution)/shard_map/late/pallas_call | solution.py:344
Async XLA Ops:
  5.0 22.6 %all-to-all-start = ((f32[128,4,128]{2,1,0:T(4,128)}), f32[128,4,128]{2,1,0:T(4,128)S(1)}, u32[]{:S(2)}, u32[]{:S(2)}) async-start(f32[128,4,128]{2,1,0:T(4,128)} %bitcast.19), calls=%async_computation | async-start | bytes 524288 | tf_op jit(solution)/shard_map/all_to_all | solution.py:286
  27.6 0.7 %copy-start = (f32[32,128]{1,0:T(8,128)S(1)}, f32[32,128]{1,0:T(8,128)}, u32[]{:S(2)}) copy-start(f32[32,128]{1,0:T(8,128)} %get-tuple-element.12.hot_ref) | copy-start | bytes 49156
  29.5 20.9 %all-to-all-start.1 = ((f32[128,8,128]{2,1,0:T(8,128)}), f32[128,8,128]{2,1,0:T(8,128)}, u32[]{:S(2)}, u32[]{:S(2)}) async-start(f32[128,8,128]{2,1,0:T(8,128)} %bitcast.9), calls=%async_computation.1 | async-start | bytes 1048576 | tf_op jit(solution)/shard_map/all_to_all | solution.py:321
